TPU v7x, 32 devices: a whole 2x2x4 slice. The times are simulated.
32 devices in a mesh: groups: 2 (over x), dp: 16 (over z, y, core).
Axes of the slice: x: 2, y: 2, z: 4, core: 2. Of those that a mesh axis runs over, the one named last changes fastest.
Arguments:
- clips: bfloat16 [128, 4, 49, 1024], P(('groups', 'dp')), parts along dimension 0, may hold values from -6 to 6
- sign_seeds: int32 [128], P(('groups', 'dp')), parts along dimension 0, may hold values from 0 to 999999
- time_weight: bfloat16 [3, 1024, 1024], replicated, may hold values from -0.109375 to 0.109375
- proj_weight: bfloat16 [1024, 512], replicated, may hold values from -0.1875 to 0.1875
- captions: bfloat16 [640, 512], P(('groups', 'dp')), parts along dimension 0, may hold values from -6 to 6
- caption_rows: int32 [128, 5], P(('groups', 'dp')), parts along dimension 0, may hold values from 0 to 319, as said below
Outputs:
- new_delta: bfloat16 [128, 4, 49, 1024], P(('groups', 'dp')), parts along dimension 0
- clip_loss: float32 [128], P(('groups', 'dp')), parts along dimension 0
There are 2 independent parts, one for each index of `groups`. A program takes and returns all parts, laid end to end along the dimension named above; an argument that names none is the same for every part. Nothing has to cross between parts.
Inputs may be any that keep to these rules, and one draw needn't show every extreme that they name: `caption_rows`: the captions of the clips of one dp device are the 20 caption rows of that device; every caption row belongs to exactly one clip.
All inputs are finite; a program needn't handle non-finite values.
Results may differ from a plain program's by a relative error of at most 0.008.
Values may be sent and summed in bfloat16 or wider, within the bound.
No kernel may reach another device: no remote copies, remote signals or barrier semaphores. Data moves between devices by JAX's collectives and lax.ppermute only.
A program may use at most 64 MiB of HBM per device.

v0:
```python
import jax
import jax.numpy as jnp
from jax import lax
from jax.sharding import PartitionSpec as P

INV_TEMP = 1.0 / 0.07


def sign_field(seeds, frames, pix, chans):
    first = lax.broadcasted_iota(jnp.int32, (frames, pix, chans), 0)
    second = lax.broadcasted_iota(jnp.int32, (frames, pix, chans), 1)
    third = lax.broadcasted_iota(jnp.int32, (frames, pix, chans), 2)
    position = (first * pix + second) * chans + third
    mixed = seeds[:, None, None, None] * jnp.int32(-1640531535) + position[None] * jnp.int32(
        374761393
    )
    mixed = mixed ^ mixed >> 13
    mixed = mixed * jnp.int32(668265263)
    mixed = mixed ^ mixed >> 16
    chosen = mixed >> 7 & 1
    return 0.1 * (2 * chosen - 1).astype(jnp.float32)


def temporal(inputs, time_weight):
    frames = inputs.shape[1]
    chans = inputs.shape[3]
    padded = jnp.pad(inputs, ((0, 0), (1, 1), (0, 0), (0, 0)))
    result = jnp.zeros(inputs.shape, jnp.float32)
    for k in range(3):
        window = padded[:, k : k + frames].reshape(-1, chans)
        result = result + jnp.dot(
            window, time_weight[k], preferred_element_type=jnp.float32
        ).reshape(inputs.shape)
    return result


def temporal_back(grad_pre, time_weight):
    frames = grad_pre.shape[1]
    chans = grad_pre.shape[3]
    padded = jnp.pad(grad_pre, ((0, 0), (1, 1), (0, 0), (0, 0)))
    result = jnp.zeros(grad_pre.shape, jnp.float32)
    for k in range(3):
        window = padded[:, 2 - k : 2 - k + frames].reshape(-1, chans)
        result = result + jnp.dot(
            window, time_weight[k].T, preferred_element_type=jnp.float32
        ).reshape(grad_pre.shape)
    return result


def gelu_tanh(value):
    return jax.nn.gelu(value, approximate=True)


def shards(clips, sign_seeds, time_weight, proj_weight, captions, caption_rows):
    clip_dev, frames, pix, chans = clips.shape
    caps_dev = captions.shape[0]
    delta0 = sign_field(sign_seeds, frames, pix, chans)
    inputs = (clips.astype(jnp.float32) + delta0).astype(jnp.bfloat16)
    pre = temporal(inputs, time_weight)
    active, act_back = jax.vjp(gelu_tanh, pre)
    pooled = jnp.mean(active, axis=(1, 2)).astype(jnp.bfloat16)
    video = jnp.dot(pooled, proj_weight, preferred_element_type=jnp.float32)
    vnorm = jnp.sqrt(jnp.sum(video * video, axis=1, keepdims=True) + 1e-06)
    vunit = video / vnorm
    video_hat = vunit.astype(jnp.bfloat16)
    cap32 = captions.astype(jnp.float32)
    caption_hat = (cap32 / jnp.sqrt(jnp.sum(cap32 * cap32, axis=1, keepdims=True) + 1e-06)).astype(
        jnp.bfloat16
    )
    local_rows = caption_rows - lax.axis_index("dp") * caps_dev
    mine = jnp.arange(caps_dev, dtype=jnp.int32)
    own = jnp.sum((local_rows[:, :, None] == mine[None, None, :]).astype(jnp.float32), axis=1)
    block_scores = (
        jnp.dot(
            caption_hat,
            lax.all_gather(video_hat, "dp", axis=0, tiled=True).T,
            preferred_element_type=jnp.float32,
        )
        * INV_TEMP
    )
    colsum = jnp.sum(jnp.exp(block_scores), axis=1)
    scaled = (caption_hat.astype(jnp.float32) / colsum[:, None]).astype(jnp.bfloat16)
    unit_piece = lax.all_gather(caption_hat, "dp", axis=0, tiled=True)
    scaled_piece = lax.all_gather(scaled, "dp", axis=0, tiled=True)
    block_scores = jnp.dot(video_hat, unit_piece.T, preferred_element_type=jnp.float32) * INV_TEMP
    block_expo = jnp.exp(block_scores)
    block_weights = block_expo.astype(jnp.bfloat16)
    total = jnp.sum(block_expo, axis=1)
    a_sum = jnp.dot(block_weights, unit_piece, preferred_element_type=jnp.float32)
    b_sum = jnp.dot(block_weights, scaled_piece, preferred_element_type=jnp.float32)
    local_scores = jnp.dot(video_hat, caption_hat.T, preferred_element_type=jnp.float32) * INV_TEMP
    local_expo = jnp.exp(local_scores)
    positive = jnp.sum(own * local_expo, axis=1)
    text_part = jnp.sum(own * (jnp.log(colsum)[None, :] - local_scores), axis=1)
    clip_loss = jnp.log(total) - jnp.log(positive) + 0.2 * text_part
    pos_sum = jnp.dot(
        (own * local_expo).astype(jnp.bfloat16), caption_hat, preferred_element_type=jnp.float32
    )
    own_sum = jnp.dot(own.astype(jnp.bfloat16), caption_hat, preferred_element_type=jnp.float32)
    grad = INV_TEMP * (
        a_sum / total[:, None] - pos_sum / positive[:, None] + 0.2 * (b_sum - own_sum)
    )
    grad_video = ((grad - vunit * jnp.sum(vunit * grad, axis=1, keepdims=True)) / vnorm).astype(
        jnp.bfloat16
    )
    grad_pooled = jnp.dot(grad_video, proj_weight.T, preferred_element_type=jnp.float32)
    spread = jnp.broadcast_to(grad_pooled[:, None, None, :] / (frames * pix), pre.shape)
    grad_pre = act_back(spread)[0].astype(jnp.bfloat16)
    grad_in = temporal_back(grad_pre, time_weight)
    rms = jnp.sqrt(jnp.mean(grad_in * grad_in, axis=(1, 2, 3), keepdims=True) + 1e-06)
    new_delta = (delta0 + grad_in / rms).astype(jnp.bfloat16)
    return (new_delta, clip_loss)


def solution(mesh):
    in_specs = (
        P(("groups", "dp"), None, None, None),
        P(("groups", "dp")),
        P(),
        P(),
        P(("groups", "dp"), None),
        P(("groups", "dp"), None),
    )
    out_specs = (P(("groups", "dp"), None, None, None), P(("groups", "dp")))
    return jax.shard_map(shards, mesh=mesh, in_specs=in_specs, out_specs=out_specs, check_vma=False)
```

profile of v0, /device:TPU:0, one launch (start us, length us, event | category | flops | bytes accessed | tf_op | source)
XLA Modules:
  0.0 102.4 jit_solution(11251730279128082261)
XLA Ops:
  0.6 0.7 broadcast_multiply_fusion.2
  1.4 0.9 fusion.45
  2.3 0.7 broadcast_subtract_fusion
  3.0 0.1 copy.15
  3.1 0.1 convert_reduce_fusion
  3.1 0.8 fusion.46
  4.0 0.8 fusion.80
  4.8 24.1 %all-gather = bf16[16,20,512]{2,1,0:T(8,128)(2,1)S(1)} all-gather(bf16[1,20,512]{2,1,0:T(8,128)(2,1)S(1)} %fusion.80), channel_id=1, replica_groups=mesh['groups'=2,'dp'=16] {'dp'}, dimensions={0}, use_global_device_ids=true | all-gather | bytes 348160 | tf_op jit(solution)/shard_map/all_gather | solution.py:83
  28.9 0.1 reshape.72
  29.0 0.2 add_multiply_fusion.1
  29.2 5.5 %fusion.18 = f32[4,4,49,1024]{3,2,1,0:T(8,128)S(1)} fusion(bf16[3,1024,1024]{2,1,0:T(8,128)(2,1)} %param.8, bf16[4,4,49,1024]{3,1,2,0:T(4,128)(2,1)} %param.6, s32[4,49,1024]{2,1,0:T(8,128)S(1)} %add_multiply_fusion.1, s32[4]{0:T(128)S(1)} %broadcast_multiply_fusion.2), kind=kOutput, calls=%fused_computation.28 | convolution fusion | flops 1245167616 | bytes 7716880 | tf_op jit(solution)/shard_map/dot_general | solution.py:31
  34.8 3.0 %fusion.22 = f32[4,4,49,1024]{3,2,1,0:T(8,128)S(1)} fusion(bf16[3,1024,1024]{2,1,0:T(8,128)(2,1)S(1)} %bitcast.54, bf16[4,4,49,1024]{3,1,2,0:T(4,128)(2,1)S(1)} %copy-done.2, s32[4,49,1024]{2,1,0:T(8,128)S(1)} %add_multiply_fusion.1, s32[4]{0:T(128)S(1)} %broadcast_multiply_fusion.2), kind=kOutput, calls=%fused_computation.32 | convolution fusion | flops 1245167616 | bytes 7832064 | tf_op jit(solution)/shard_map/dot_general | solution.py:31
  37.8 6.3 %fusion.15 = (f32[4,1024]{1,0:T(4,128)S(1)}, f32[4,4,49,1024]{3,2,1,0:T(8,128)}) fusion(f32[4,4,49,1024]{3,2,1,0:T(8,128)S(1)} %fusion.22, f32[4,4,49,1024]{3,2,1,0:T(8,128)S(1)} %fusion.18, bf16[3,1024,1024]{2,1,0:T(8,128)(2,1)S(1)} %bitcast.54, bf16[4,4,49,1024]{3,1,2,0:T(4,128)(2,1)S(1)} %copy-done.2, s32[4,49,1024]{2,1,0:T(8,128)S(1)} %add_multiply_fusion.1, ...), kind=kOutput, calls=%fused_computation.23 | convolution fusion | flops 1665036288 | bytes 15188480 | tf_op jit(solution)/shard_map/dot_general | solution.py:31
  44.2 0.4 multiply_reduce_fusion.2
  44.5 0.3 fusion.67
  44.9 0.2 convolution_divide_fusion.1
  45.0 0.1 convert_bitcast_fusion
  45.1 17.6 %all-gather.1 = bf16[16,4,512]{2,1,0:T(4,128)(2,1)S(1)} all-gather(bf16[1,4,512]{2,1,0:T(4,128)(2,1)S(1)} %convert_bitcast_fusion), channel_id=1, replica_groups=mesh['groups'=2,'dp'=16] {'dp'}, dimensions={0}, use_global_device_ids=true | all-gather | bytes 69632 | tf_op jit(solution)/shard_map/all_gather | solution.py:76
  62.7 0.2 fusion.43
  63.0 0.3 multiply_reduce_fusion.3
  63.3 0.5 multiply_add_fusion
  63.8 0.1 fusion.42
  63.9 0.1 fusion.47
  64.0 20.1 %all-gather.2 = bf16[16,20,512]{2,1,0:T(8,128)(2,1)S(1)} all-gather(bf16[1,20,512]{2,1,0:T(8,128)(2,1)S(1)} %fusion.47), channel_id=1, replica_groups=mesh['groups'=2,'dp'=16] {'dp'}, dimensions={0}, use_global_device_ids=true | all-gather | bytes 348160 | tf_op jit(solution)/shard_map/all_gather | solution.py:84
  84.2 0.1 fusion.55
  84.3 0.2 multiply_reduce_fusion.1
  84.6 0.4 broadcast_multiply_fusion
  85.0 5.8 %fusion.16 = f32[4,4,49,1024]{3,2,1,0:T(8,128)S(1)} fusion(bf16[3,1024,1024]{2,1,0:T(8,128)(2,1)} %param.8, f32[4,4,49,1024]{3,2,1,0:T(8,128)} %get-tuple-element.15, f32[4,1024]{1,0:T(4,128)S(1)} %get-tuple-element.13, f32[4,1024]{1,0:T(4,128)S(1)} %get-tuple-element.12), kind=kOutput, calls=%fused_computation.26 | convolution fusion | flops 1248378880 | bytes 9011200 | tf_op jit(solution)/shard_map/dot_general | solution.py:44
  90.8 3.2 %fusion.20 = f32[4,4,49,1024]{3,2,1,0:T(8,128)S(1)} fusion(bf16[3,1024,1024]{2,1,0:T(8,128)(2,1)S(1)} %bitcast.56, f32[4,4,49,1024]{3,2,1,0:T(8,128)S(1)} %copy-done.3, f32[4,1024]{1,0:T(4,128)S(1)} %get-tuple-element.13, f32[4,1024]{1,0:T(4,128)S(1)} %get-tuple-element.12), kind=kOutput, calls=%fused_computation.30 | convolution fusion | flops 1248378880 | bytes 9011200 | tf_op jit(solution)/shard_map/dot_general | solution.py:44
  94.1 4.1 %multiply_reduce_fusion = (f32[4]{0:T(128)S(1)}, f32[4,4,49,1024]{3,2,1,0:T(8,128)S(1)}) fusion(f32[4,4,49,1024]{3,2,1,0:T(8,128)S(1)} %fusion.20, f32[4,4,49,1024]{3,2,1,0:T(8,128)S(1)} %fusion.16, bf16[3,1024,1024]{2,1,0:T(8,128)(2,1)S(1)} %bitcast.56, f32[4,4,49,1024]{3,2,1,0:T(8,128)S(1)} %copy-done.3, f32[4,1024]{1,0:T(4,128)S(1)} %get-tuple-element.13, ...), kind=kOutput, calls=%fused_computation.19 | convolution fusion | flops 1662631936 | bytes 16351248 | tf_op jit(solution)/shard_map/dot_general | solution.py:44
  98.2 1.8 %add_convert_fusion = bf16[4,4,49,1024]{3,2,1,0:T(8,128)(2,1)S(1)} fusion(f32[4,4,49,1024]{3,2,1,0:T(8,128)S(1)} %get-tuple-element.24, f32[4]{0:T(128)S(1)} %add_sqrt_fusion, s32[4,49,1024]{2,1,0:T(8,128)S(1)} %add_multiply_fusion.1, s32[4]{0:T(128)S(1)} %broadcast_multiply_fusion.2), kind=kLoop, calls=%fused_computation.18 | loop fusion | flops 12042240 | bytes 5619744 | tf_op jit(solution)/shard_map/convert_element_type | solution.py:111
  100.0 2.4 %copy.16 = bf16[4,4,49,1024]{3,1,2,0:T(4,128)(2,1)} copy(bf16[4,4,49,1024]{3,2,1,0:T(8,128)(2,1)S(1)} %add_convert_fusion) | data formatting | bytes 3211264
  (25 shorter events, 0.2 us)
Async XLA Ops:
  0.6 43.5 %copy-start = (bf16[1024,512]{1,0:T(8,128)(2,1)S(1)}, bf16[1024,512]{1,0:T(8,128)(2,1)}, u32[]{:S(2)}) copy-start(bf16[1024,512]{1,0:T(8,128)(2,1)} %param.9) | copy-start | bytes 3145732
  29.0 5.8 %slice-start = ((s8[6291456]{0:T(1024)(128)(4,1)}), s8[4194304]{0:T(1024)(128)(4,1)S(1)}, s32[]{:S(2)}) async-start(s8[6291456]{0:T(1024)(128)(4,1)} %bitcast.53), calls=%async_computation | async-start | bytes 8388608
  29.2 5.6 %slice-start.1 = ((s8[6291456]{0:T(1024)(128)(4,1)}), s8[2097152]{0:T(1024)(128)(4,1)S(1)}, s32[]{:S(2)}) async-start(s8[6291456]{0:T(1024)(128)(4,1)} %bitcast.53), calls=%async_computation.1 | async-start | bytes 4194304
  29.2 5.6 %copy-start.2 = (bf16[4,4,49,1024]{3,1,2,0:T(4,128)(2,1)S(1)}, bf16[4,4,49,1024]{3,1,2,0:T(4,128)(2,1)}, u32[]{:S(2)}) copy-start(bf16[4,4,49,1024]{3,1,2,0:T(4,128)(2,1)} %param.6) | copy-start | bytes 4816900
  37.8 26.1 %copy-start.1 = (bf16[20,512]{1,0:T(8,128)(2,1)S(1)}, bf16[20,512]{1,0:T(8,128)(2,1)}, u32[]{:S(2)}) copy-start(bf16[20,512]{1,0:T(8,128)(2,1)} %param.10) | copy-start | bytes 61444
  84.6 6.2 %slice-start.2 = ((s8[6291456]{0:T(1024)(128)(4,1)}), s8[4194304]{0:T(1024)(128)(4,1)S(1)}, s32[]{:S(2)}) async-start(s8[6291456]{0:T(1024)(128)(4,1)} %bitcast.55), calls=%async_computation.2 | async-start | bytes 8388608
  85.0 5.8 %slice-start.3 = ((s8[6291456]{0:T(1024)(128)(4,1)}), s8[2097152]{0:T(1024)(128)(4,1)S(1)}, s32[]{:S(2)}) async-start(s8[6291456]{0:T(1024)(128)(4,1)} %bitcast.55), calls=%async_computation.3 | async-start | bytes 4194304
  85.0 5.8 %copy-start.3 = (f32[4,4,49,1024]{3,2,1,0:T(8,128)S(1)}, f32[4,4,49,1024]{3,2,1,0:T(8,128)}, u32[]{:S(2)}) copy-start(f32[4,4,49,1024]{3,2,1,0:T(8,128)} %get-tuple-element.15) | copy-start | bytes 9633796
where the time goes:
time: 103 us; the launch traced here: 102 us
  blocking collectives  61.8 us (60%)
  matrix products  30.3 us (29%)
  other arithmetic  6.73 us (7%)
  local copies, waits for them, and re-layouts  2.72 us (3%)
    all_gather x1, blocking collectives, shards(): unit_piece = lax.all_gather(caption_hat, 'dp', axis=0, tiled=True)  24.1 us
    all_gather x1, blocking collectives, shards(): scaled_piece = lax.all_gather(scaled, 'dp', axis=0, tiled=True)  20.1 us
    all_gather x1, blocking collectives, shards(): lax.all_gather(video_hat, 'dp', axis=0, tiled=True)  17.6 us
    dot_general x3, matrix products, temporal(): jnp.dot(window, time_weight[k], preferred_element_type=jnp.float32)  14.9 us
    dot_general x3, matrix products, temporal_back(): jnp.dot(window, time_weight[k].T, preferred_element_type=jnp.float32)  13.1 us
    unnamed x20, local copies, waits for them, and re-layouts  2.62 us

commit v1 on v0

--- a/solution.py
+++ b/solution.py
@@ -80,8 +80,11 @@
     )
     colsum = jnp.sum(jnp.exp(block_scores), axis=1)
     scaled = (caption_hat.astype(jnp.float32) / colsum[:, None]).astype(jnp.bfloat16)
-    unit_piece = lax.all_gather(caption_hat, "dp", axis=0, tiled=True)
-    scaled_piece = lax.all_gather(scaled, "dp", axis=0, tiled=True)
+    unit_piece, scaled_piece = jnp.split(
+        lax.all_gather(jnp.concatenate([caption_hat, scaled], axis=1), "dp", axis=0, tiled=True),
+        [caption_hat.shape[1]],
+        axis=1,
+    )
     block_scores = jnp.dot(video_hat, unit_piece.T, preferred_element_type=jnp.float32) * INV_TEMP
     block_expo = jnp.exp(block_scores)
     block_weights = block_expo.astype(jnp.bfloat16)

time: 103 us -> 82.9 us (0.80)
  blocking collectives: 61.8 us -> 43 us
    all_gather x2 -> x1, blocking collectives: 44.2 us -> 19.8 us  [shards(): lax.all_gather(jnp.concatenate([caption_hat, scaled], axis=1), 'dp', axis...]
    all_gather x1, blocking collectives: 17.6 us -> 23.3 us  [shards(): lax.all_gather(video_hat, 'dp', axis=0, tiled=True)]
    unnamed x20 -> x19, local copies, waits for them, and re-layouts: 2.62 us -> 2.61 us
where the time goes in v1:
time: 82.9 us; the launch traced here: 82.6 us
  blocking collectives  43 us (52%)
  matrix products  30.1 us (36%)
  other arithmetic  5.93 us (7%)
  local copies, waits for them, and re-layouts  2.71 us (3%)
  between operations  0.84 us (1%)
    all_gather x1, blocking collectives, shards(): lax.all_gather(video_hat, 'dp', axis=0, tiled=True)  23.3 us
    all_gather x1, blocking collectives, shards(): lax.all_gather(jnp.concatenate([caption_hat, scaled], axis=1), 'dp', axis...  19.8 us
    dot_general x3, matrix products, temporal(): jnp.dot(window, time_weight[k], preferred_element_type=jnp.float32)  14.8 us
    dot_general x3, matrix products, temporal_back(): jnp.dot(window, time_weight[k].T, preferred_element_type=jnp.float32)  13 us
    unnamed x19, local copies, waits for them, and re-layouts  2.61 us
    convert_element_type x1, other arithmetic, shards(): new_delta = (delta0 + grad_in / rms).astype(jnp.bfloat16)  1.83 us

profile of v1, /device:TPU:0, one launch (start us, length us, event | category | flops | bytes accessed | tf_op | source)
XLA Modules:
  0.0 82.6 jit_solution(12380686003961418188)
XLA Ops:
  0.6 0.0 copy-start
  0.6 0.7 broadcast_multiply_fusion.2
  1.4 0.9 %fusion.49 = f32[20]{0:T(128)S(1)} fusion(bf16[20,512]{1,0:T(8,128)(2,1)} %param.10), kind=kLoop, calls=%fused_computation.64 | loop fusion | flops 30700 | bytes 20560 | tf_op jit(solution)/shard_map/reduce_sum | solution.py:67
  2.3 0.7 broadcast_subtract_fusion
  3.0 0.1 copy.15
  3.1 0.1 convert_reduce_fusion
  3.1 0.8 fusion.50
  4.0 0.2 add_multiply_fusion.1
  4.1 0.0 slice-start.1
  4.2 5.5 %fusion.18 = f32[4,4,49,1024]{3,2,1,0:T(8,128)S(1)} fusion(bf16[3,1024,1024]{2,1,0:T(8,128)(2,1)} %param.8, bf16[4,4,49,1024]{3,1,2,0:T(4,128)(2,1)} %param.6, s32[4,49,1024]{2,1,0:T(8,128)S(1)} %add_multiply_fusion.1, s32[4]{0:T(128)S(1)} %broadcast_multiply_fusion.2), kind=kOutput, calls=%fused_computation.28 | convolution fusion | flops 1245167616 | bytes 7716880 | tf_op jit(solution)/shard_map/dot_general | solution.py:31
  9.7 3.0 %fusion.22 = f32[4,4,49,1024]{3,2,1,0:T(8,128)S(1)} fusion(bf16[3,1024,1024]{2,1,0:T(8,128)(2,1)S(1)} %bitcast.49, bf16[4,4,49,1024]{3,1,2,0:T(4,128)(2,1)S(1)} %copy-done.2, s32[4,49,1024]{2,1,0:T(8,128)S(1)} %add_multiply_fusion.1, s32[4]{0:T(128)S(1)} %broadcast_multiply_fusion.2), kind=kOutput, calls=%fused_computation.32 | convolution fusion | flops 1245167616 | bytes 7832064 | tf_op jit(solution)/shard_map/dot_general | solution.py:31
  12.7 6.3 %fusion.15 = (f32[4,1024]{1,0:T(4,128)S(1)}, f32[4,4,49,1024]{3,2,1,0:T(8,128)}) fusion(f32[4,4,49,1024]{3,2,1,0:T(8,128)S(1)} %fusion.22, f32[4,4,49,1024]{3,2,1,0:T(8,128)S(1)} %fusion.18, bf16[3,1024,1024]{2,1,0:T(8,128)(2,1)S(1)} %bitcast.49, bf16[4,4,49,1024]{3,1,2,0:T(4,128)(2,1)S(1)} %copy-done.2, s32[4,49,1024]{2,1,0:T(8,128)S(1)} %add_multiply_fusion.1, ...), kind=kOutput, calls=%fused_computation.23 | convolution fusion | flops 1665036288 | bytes 15188480 | tf_op jit(solution)/shard_map/dot_general | solution.py:31
  19.0 0.4 multiply_reduce_fusion.2
  19.4 0.1 convert_bitcast_fusion
  19.5 23.3 %all-gather = bf16[16,4,512]{2,1,0:T(4,128)(2,1)S(1)} all-gather(bf16[1,4,512]{2,1,0:T(4,128)(2,1)S(1)} %convert_bitcast_fusion), channel_id=1, replica_groups=mesh['groups'=2,'dp'=16] {'dp'}, dimensions={0}, use_global_device_ids=true | all-gather | bytes 69632 | tf_op jit(solution)/shard_map/all_gather | solution.py:76
  42.7 0.2 fusion.43
  43.0 0.3 multiply_reduce_fusion.3
  43.3 0.1 divide_convert_fusion
  43.4 19.8 %all-gather.1 = bf16[16,20,1024]{2,1,0:T(8,128)(2,1)S(1)} all-gather(bf16[1,20,1024]{2,1,0:T(8,128)(2,1)S(1)} %maximum_bitcast_fusion), channel_id=1, replica_groups=mesh['groups'=2,'dp'=16] {'dp'}, dimensions={0}, use_global_device_ids=true | all-gather | bytes 696320 | tf_op jit(solution)/shard_map/all_gather | solution.py:84
  63.2 0.1 reshape.74
  63.3 0.3 fusion.69
  63.7 0.5 multiply_add_fusion
  64.2 0.2 convolution_divide_fusion.1
  64.4 0.2 fusion.45
  64.5 0.1 fusion.42
  64.6 0.2 multiply_reduce_fusion.1
  64.9 0.4 broadcast_multiply_fusion
  65.3 5.8 %fusion.16 = f32[4,4,49,1024]{3,2,1,0:T(8,128)S(1)} fusion(bf16[3,1024,1024]{2,1,0:T(8,128)(2,1)} %param.8, f32[4,4,49,1024]{3,2,1,0:T(8,128)} %get-tuple-element.15, f32[4,1024]{1,0:T(4,128)S(1)} %get-tuple-element.13, f32[4,1024]{1,0:T(4,128)S(1)} %get-tuple-element.12), kind=kOutput, calls=%fused_computation.26 | convolution fusion | flops 1248378880 | bytes 9011200 | tf_op jit(solution)/shard_map/dot_general | solution.py:44
  71.1 3.2 %fusion.20 = f32[4,4,49,1024]{3,2,1,0:T(8,128)S(1)} fusion(bf16[3,1024,1024]{2,1,0:T(8,128)(2,1)S(1)} %bitcast.51, f32[4,4,49,1024]{3,2,1,0:T(8,128)S(1)} %copy-done.3, f32[4,1024]{1,0:T(4,128)S(1)} %get-tuple-element.13, f32[4,1024]{1,0:T(4,128)S(1)} %get-tuple-element.12), kind=kOutput, calls=%fused_computation.30 | convolution fusion | flops 1248378880 | bytes 9011200 | tf_op jit(solution)/shard_map/dot_general | solution.py:44
  74.3 4.0 %multiply_reduce_fusion = (f32[4]{0:T(128)S(1)}, f32[4,4,49,1024]{3,2,1,0:T(8,128)S(1)}) fusion(f32[4,4,49,1024]{3,2,1,0:T(8,128)S(1)} %fusion.20, f32[4,4,49,1024]{3,2,1,0:T(8,128)S(1)} %fusion.16, bf16[3,1024,1024]{2,1,0:T(8,128)(2,1)S(1)} %bitcast.51, f32[4,4,49,1024]{3,2,1,0:T(8,128)S(1)} %copy-done.3, f32[4,1024]{1,0:T(4,128)S(1)} %get-tuple-element.13, ...), kind=kOutput, calls=%fused_computation.19 | convolution fusion | flops 1662631936 | bytes 16351248 | tf_op jit(solution)/shard_map/dot_general | solution.py:44
  78.3 1.8 %add_convert_fusion = bf16[4,4,49,1024]{3,2,1,0:T(8,128)(2,1)S(1)} fusion(f32[4,4,49,1024]{3,2,1,0:T(8,128)S(1)} %get-tuple-element.24, f32[4]{0:T(128)S(1)} %add_sqrt_fusion, s32[4,49,1024]{2,1,0:T(8,128)S(1)} %add_multiply_fusion.1, s32[4]{0:T(128)S(1)} %broadcast_multiply_fusion.2), kind=kLoop, calls=%fused_computation.18 | loop fusion | flops 12042240 | bytes 5619744 | tf_op jit(solution)/shard_map/convert_element_type | solution.py:114
  80.2 2.4 %copy.16 = bf16[4,4,49,1024]{3,1,2,0:T(4,128)(2,1)} copy(bf16[4,4,49,1024]{3,2,1,0:T(8,128)(2,1)S(1)} %add_convert_fusion) | data formatting | bytes 3211264
  (23 shorter events, 0.1 us)
Async XLA Ops:
  0.6 18.4 %copy-start = (bf16[1024,512]{1,0:T(8,128)(2,1)S(1)}, bf16[1024,512]{1,0:T(8,128)(2,1)}, u32[]{:S(2)}) copy-start(bf16[1024,512]{1,0:T(8,128)(2,1)} %param.9) | copy-start | bytes 3145732
  4.0 5.7 %slice-start = ((s8[6291456]{0:T(1024)(128)(4,1)}), s8[4194304]{0:T(1024)(128)(4,1)S(1)}, s32[]{:S(2)}) async-start(s8[6291456]{0:T(1024)(128)(4,1)} %bitcast.48), calls=%async_computation | async-start | bytes 8388608
  4.1 5.6 %slice-start.1 = ((s8[6291456]{0:T(1024)(128)(4,1)}), s8[2097152]{0:T(1024)(128)(4,1)S(1)}, s32[]{:S(2)}) async-start(s8[6291456]{0:T(1024)(128)(4,1)} %bitcast.48), calls=%async_computation.1 | async-start | bytes 4194304
  4.2 5.6 %copy-start.2 = (bf16[4,4,49,1024]{3,1,2,0:T(4,128)(2,1)S(1)}, bf16[4,4,49,1024]{3,1,2,0:T(4,128)(2,1)}, u32[]{:S(2)}) copy-start(bf16[4,4,49,1024]{3,1,2,0:T(4,128)(2,1)} %param.6) | copy-start | bytes 4816900
  12.7 30.6 %copy-start.1 = (bf16[20,512]{1,0:T(8,128)(2,1)S(1)}, bf16[20,512]{1,0:T(8,128)(2,1)}, u32[]{:S(2)}) copy-start(bf16[20,512]{1,0:T(8,128)(2,1)} %param.10) | copy-start | bytes 61444
  64.9 6.2 %slice-start.2 = ((s8[6291456]{0:T(1024)(128)(4,1)}), s8[4194304]{0:T(1024)(128)(4,1)S(1)}, s32[]{:S(2)}) async-start(s8[6291456]{0:T(1024)(128)(4,1)} %bitcast.50), calls=%async_computation.2 | async-start | bytes 8388608
  65.3 5.8 %slice-start.3 = ((s8[6291456]{0:T(1024)(128)(4,1)}), s8[2097152]{0:T(1024)(128)(4,1)S(1)}, s32[]{:S(2)}) async-start(s8[6291456]{0:T(1024)(128)(4,1)} %bitcast.50), calls=%async_computation.3 | async-start | bytes 4194304
  65.3 5.8 %copy-start.3 = (f32[4,4,49,1024]{3,2,1,0:T(8,128)S(1)}, f32[4,4,49,1024]{3,2,1,0:T(8,128)}, u32[]{:S(2)}) copy-start(f32[4,4,49,1024]{3,2,1,0:T(8,128)} %get-tuple-element.15) | copy-start | bytes 9633796
